TPU v7x, 128 devices: a whole 4x4x4 slice. The times are simulated.
128 devices in a mesh: section: 8 (over z, x_lo), tp: 16 (over y, x_hi, core).
Axes of the slice: x: 4 (x_hi: 2, x_lo: 2; x = x_hi * 2 + x_lo), y: 4, z: 4, core: 2. Of those that a mesh axis runs over, the one named last changes fastest.
Arguments:
- teacher_rows: bfloat16 [8, 256, 8192], P('section', 'tp'), may hold values from -72 to 72
- norm_gain: float32 [8, 8192], P('section'), may hold values from 0.1 to 1.9
- query_weight: bfloat16 [8, 8192, 8192], P('section', None, 'tp'), may hold values from -2.762136 to 2.762136
- keys_values: bfloat16 [8, 2, 8192, 1024], P('section', None, None, 'tp'), may hold values from -0.071815532 to 0.071815532
- output_weight: bfloat16 [8, 8192, 8192], P('section', 'tp'), may hold values from -0.5 to 0.5
- doc_start: int32 [8], P('section'), may hold values from 1 to 255
- student_rows: bfloat16 [8, 256, 4096], P('section', 'tp'), may hold values from -30 to 30
- projector: bfloat16 [4096, 8192], P('tp', 'section'), may hold values from -1 to 2
Outputs:
- teacher_next: bfloat16 [8, 256, 8192], P('section', 'tp')
- distill_loss: float32 [], replicated
- grad_student: float32 [8, 256, 4096], P('section', 'tp')
- grad_projector: float32 [4096, 8192], P('tp', 'section')
All inputs are finite; a program needn't handle non-finite values.
Results may differ from a plain program's by a relative error of at most 0.02.
Values may be sent and summed in bfloat16 or wider, within the bound.
No kernel may reach another device: no remote copies, remote signals or barrier semaphores. Data moves between devices by JAX's collectives and lax.ppermute only.
A program may use at most 128 MiB of HBM per device.

v0:
```python
import math
import jax
import jax.numpy as jnp
from jax import lax
from jax.sharding import PartitionSpec as P

HD = 128
LOSS_WEIGHT = 64.0
NORM_EPS = 1e-05
COS_EPS = 1e-06


def partner(value, axis, apart):
    mask = 2**apart
    pairs = [(source, source ^ mask) for source in range(lax.axis_size(axis))]
    return lax.ppermute(value, axis, pairs)


def from_everyone(value, axis):
    copies = jnp.broadcast_to(value, (lax.axis_size(axis), *value.shape))
    return lax.all_to_all(copies, axis, split_axis=0, concat_axis=0, tiled=True)


def laid_out(pieces, dim):
    pieces = jnp.moveaxis(pieces, 0, dim)
    shape = pieces.shape
    return pieces.reshape(*shape[:dim], shape[dim] * shape[dim + 1], *shape[dim + 2 :])


def collect(value, axis, dim):
    pieces = from_everyone(value, axis)
    return laid_out(pieces, dim)


def taken_together(value, axis):
    everything = from_everyone(value, axis)
    return jnp.sum(everything, axis=0)


def packed_total(arrays, axis):
    ends = [0]
    for a in arrays:
        ends.append(ends[-1] + a.size)
    subtotal = taken_together(jnp.concatenate([a.ravel() for a in arrays]), axis)
    return tuple((subtotal[b:e].reshape(a.shape) for a, b, e in zip(arrays, ends, ends[1:])))


def cut_along(value, dim, length):
    shape = value.shape
    pieces = value.reshape(*shape[:dim], length, shape[dim] // length, *shape[dim + 1 :])
    return jnp.moveaxis(pieces, dim, 0)


def sent_and_summed(value, axis, dim):
    pieces = cut_along(value, dim, lax.axis_size(axis))
    arrived = lax.all_to_all(pieces, axis, split_axis=0, concat_axis=0, tiled=True)
    return arrived.astype(jnp.float32).sum(axis=0)


def round_bf16(values):
    return lax.optimization_barrier(values.astype(jnp.bfloat16)).astype(jnp.float32)


def join_halves(mine, other, low_side):
    return jnp.where(
        low_side, jnp.concatenate([mine, other], axis=1), jnp.concatenate([other, mine], axis=1)
    )


def cosine_step(inner, own_sq, target_sq, student_proj, target):
    inv_own = lax.rsqrt(own_sq + COS_EPS)
    inv_target = lax.rsqrt(target_sq + COS_EPS)
    cosine = inner * inv_own * inv_target
    slope = LOSS_WEIGHT * (
        (inner * inv_target * inv_own * inv_own * inv_own)[:, None] * student_proj
        - target * (inv_own * inv_target)[:, None]
    )
    return (cosine, slope.astype(jnp.bfloat16))


def attend(queries, keys_full, values_full, first_new):
    row_total = queries.shape[0]
    kv_heads = keys_full.shape[1] // HD
    group = queries.shape[1] // HD // kv_heads
    query_heads = queries.reshape(row_total, kv_heads, group, HD)
    key_heads = keys_full.reshape(row_total, kv_heads, HD)
    value_heads = values_full.reshape(row_total, kv_heads, HD)
    scale = 1.0 / math.sqrt(HD)
    scores = (
        jnp.einsum("qegd,ked->egqk", query_heads, key_heads, preferred_element_type=jnp.float32)
        * scale
    )
    positions = jnp.arange(row_total, dtype=jnp.int32)
    after_start = positions >= first_new
    visible = (positions[None, :] <= positions[:, None]) & (
        after_start[None, :] == after_start[:, None]
    )
    scores = jnp.where(visible, scores, -1e30)
    row_max = jnp.max(scores, axis=-1, keepdims=True)
    expo = jnp.where(visible, jnp.exp(scores - row_max), 0.0)
    weights = (expo / jnp.sum(expo, axis=-1, keepdims=True)).astype(jnp.bfloat16)
    mixed = jnp.einsum("egqk,ked->qegd", weights, value_heads, preferred_element_type=jnp.float32)
    return mixed.astype(jnp.bfloat16).reshape(row_total, queries.shape[1])


def shards(
    teacher_rows,
    norm_gain,
    query_weight,
    keys_values,
    output_weight,
    doc_start,
    student_rows,
    projector,
):
    span_rows = teacher_rows[0]
    tp_count = lax.axis_size("tp")
    tp_position = lax.axis_index("tp")
    rows_float = span_rows.astype(jnp.float32)
    mean_square = jnp.mean(rows_float * rows_float, axis=1, keepdims=True)
    normed = (rows_float * lax.rsqrt(mean_square + NORM_EPS) * norm_gain[0][None, :]).astype(
        jnp.bfloat16
    )
    query_local = query_weight[0]
    key_local = keys_values[0, 0]
    value_local = keys_values[0, 1]
    query_cols = query_local.shape[1]
    key_cols = key_local.shape[1]
    block_rows = lax.all_gather(normed, "tp", axis=0, tiled=True)
    query_part = jnp.dot(block_rows, query_local, preferred_element_type=jnp.float32).astype(
        jnp.bfloat16
    )
    key_part = jnp.dot(block_rows, key_local, preferred_element_type=jnp.float32).astype(
        jnp.bfloat16
    )
    value_part = jnp.dot(block_rows, value_local, preferred_element_type=jnp.float32).astype(
        jnp.bfloat16
    )
    projected = jnp.concatenate([query_part, key_part, value_part], axis=1)
    queries = projected[:, :query_cols]
    keys_full = projected[:, query_cols : query_cols + key_cols]
    values_full = projected[:, query_cols + key_cols :]
    other_key, other_value = partner((keys_full, values_full), "tp", 0)
    low_side = tp_position // 2**0 % 2 == 0
    keys_full = join_halves(keys_full, other_key, low_side)
    values_full = join_halves(values_full, other_value, low_side)
    mixed_heads = attend(queries, keys_full, values_full, doc_start[0])
    out_local = output_weight[0]
    block = mixed_heads
    attn_sum = lax.psum_scatter(
        round_bf16(jnp.dot(block, out_local, preferred_element_type=jnp.float32)).astype(
            jnp.bfloat16
        ),
        "tp",
        scatter_dimension=0,
        tiled=True,
    ).astype(jnp.float32)
    teacher_next = (rows_float + attn_sum).astype(jnp.bfloat16)
    contract_last = (((1,), (1,)), ((), ()))
    contract_pair = (((0, 1), (0, 1)), ((), ()))
    gathered = collect(student_rows, "section", 0)
    token_count = gathered.shape[0] * gathered.shape[1]
    token_rows = gathered.reshape(token_count, gathered.shape[2])
    arrived = lax.all_to_all(teacher_next[None], "section", split_axis=2, concat_axis=0, tiled=True)
    target = arrived.reshape(token_count, arrived.shape[2]).astype(jnp.float32)
    proj_block = lax.all_gather(projector, "tp", axis=0, tiled=True)
    student_proj = jnp.dot(token_rows, proj_block, preferred_element_type=jnp.float32)
    inner, own_sq, target_sq = packed_total(
        (
            jnp.sum(student_proj * target, axis=1),
            jnp.sum(student_proj * student_proj, axis=1),
            jnp.sum(target * target, axis=1),
        ),
        "section",
    )
    cosine, slope = cosine_step(inner, own_sq, target_sq, student_proj, target)
    loss_total = taken_together(jnp.sum(1.0 - cosine), "tp")
    distill_loss = loss_total / (token_count * tp_count)
    block = slope
    grad_local = sent_and_summed(
        lax.dot_general(
            block, proj_block, contract_last, preferred_element_type=jnp.float32
        ).astype(jnp.bfloat16),
        "section",
        0,
    )
    by_column = lax.all_to_all(gathered, "tp", split_axis=2, concat_axis=1, tiled=True)
    slope_stacked = slope.reshape(gathered.shape[0], gathered.shape[1], slope.shape[1])
    block = by_column
    grad_proj = lax.dot_general(
        block,
        lax.all_gather(slope_stacked, "tp", axis=1, tiled=True),
        contract_pair,
        preferred_element_type=jnp.float32,
    )
    return (teacher_next[None], distill_loss, grad_local[None], grad_proj)


def solution(mesh):
    placed = (
        P("section", "tp", None),
        P("section", None),
        P("section", None, "tp"),
        P("section", None, None, "tp"),
        P("section", "tp", None),
        P("section"),
        P("section", "tp", None),
        P("tp", "section"),
    )
    return jax.shard_map(
        shards,
        mesh=mesh,
        in_specs=placed,
        out_specs=(P("section", "tp", None), P(), P("section", "tp", None), P("tp", "section")),
        check_vma=False,
    )
```

profile of v0, /device:TPU:1, one launch (start us, length us, event | category | flops | bytes accessed | tf_op | source)
XLA Modules:
  0.0 376.0 jit_solution(13403994111314197012)
XLA Ops:
  7.2 1.3 fusion.16
  8.5 1.8 fusion.18
  11.2 58.2 %all-gather.4.cloned.1.call-done = bf16[256,8192]{1,0:T(8,128)(2,1)} async-done(((bf16[16,8192]{1,0:T(8,128)(2,1)}), bf16[256,8192]{1,0:T(8,128)(2,1)}) %all-gather.4.cloned.1.call-update) | async-done | bytes 4194320 | tf_op jit(solution)/shard_map/all_gather | solution.py:129
  69.4 4.0 %convolution_convert_fusion.3 = bf16[256,64]{0,1:T(8,128)(2,1)S(1)} fusion(bf16[256,8192]{1,0:T(8,128)(2,1)} %all-gather.4.cloned.1.call-done, bf16[1,2,8192,64]{2,3,1,0:T(8,128)(2,1)} %param.11), kind=kOutput, calls=%fused_computation.13 | convolution fusion | flops 268451840 | bytes 5275648 | tf_op jit(solution)/shard_map/dot_general | solution.py:133
  73.8 1.4 convolution_convert_fusion.4
  75.5 5.8 %fusion.8 = bf16[32,4,8,128]{3,2,1,0:T(8,128)(2,1)S(1)} fusion(bf16[256,8192]{1,0:T(8,128)(2,1)S(1)} %copy-done, bf16[1,8192,512]{2,1,0:T(8,128)(2,1)} %param.10), kind=kOutput, calls=%fused_computation.12 | convolution fusion | flops 2147614720 | bytes 12845056 | tf_op jit(solution)/shard_map/dot_general | solution.py:130
  82.4 4.5 %convolution_convert_fusion = bf16[256,8192]{1,0:T(8,128)(2,1)} fusion(bf16[256,512]{0,1:T(8,128)(2,1)S(1)} %bitcast.115, bf16[1,512,8192]{2,1,0:T(8,128)(2,1)S(1)} %bitcast.111), kind=kOutput, calls=%fused_computation | convolution fusion | flops 2149580800 | bytes 12845056 | tf_op jit(solution)/shard_map/dot_general | solution.py:151
  87.6 76.1 %reduce-scatter.2.cloned.1.call-done = bf16[16,8192]{1,0:T(8,128)(2,1)} async-done(((bf16[256,8192]{1,0:T(8,128)(2,1)}), bf16[16,8192]{1,0:T(8,128)(2,1)}) %reduce-scatter.2.cloned.1.call-update) | async-done | bytes 262160 | tf_op jit(solution)/shard_map/reduce_scatter | solution.py:150
  164.7 6.8 %copy.48 = bf16[1,16,8192]{1,0,2:T(2,128)(2,1)} copy(bf16[1,16,8192]{2,1,0:T(8,128)(2,1)S(1)} %fusion.26) | data formatting | bytes 524288 | tf_op jit(solution)/shard_map/broadcast_in_dim | solution.py:196
  172.0 45.2 %reduce.8 = bf16[8192,16]{1,0:T(8,128)(2,1)S(1)} reduce(bf16[8192,1,16]{2,1,0:T(2,128)(2,1)} %bitcast.106, bf16[]{:T(256)} %broadcast.68), dimensions={1}, to_apply=%bitcast.82.reduce_sub_computation | reduce | bytes 524290
  217.3 2.2 reshape.123
  219.5 10.6 %all_to_all.49 = bf16[8,2,8192]{2,1,0:T(2,128)(2,1)S(1)} all-to-all(bf16[8,2,8192]{2,1,0:T(2,128)(2,1)S(1)} %reshape.123), channel_id=1, replica_groups=mesh['section'=8,'tp'=16] {'section'}, dimensions={0} | all-to-all | bytes 524288 | tf_op jit(solution)/shard_map/all_to_all | solution.py:164
  230.1 1.1 broadcast_in_dim.41
  231.2 3.6 all-to-all-start
  234.8 5.1 %reshape.124 = bf16[8192,1,16]{2,1,0:T(2,128)(2,1)} reshape(bf16[8,2,8192]{2,1,0:T(2,128)(2,1)S(1)} %all_to_all.49) | data formatting | bytes 524288
  239.9 8.5 %convert_multiply_fusion.2 = f32[1,16,8192]{1,0,2:T(1,128)} fusion(bf16[8192,1,16]{2,1,0:T(2,128)(2,1)} %reshape.124), kind=kLoop, calls=%fused_computation.68 | loop fusion | flops 262144 | bytes 786432 | tf_op jit(solution)/shard_map/mul | solution.py:172
  248.4 2.5 reduce_sum.89
  250.9 8.5 %bitcast_convert_fusion = f32[1,16,8192]{1,0,2:T(1,128)} fusion(bf16[8192,1,16]{2,1,0:T(2,128)(2,1)} %reshape.124), kind=kLoop, calls=%fused_computation.72 | loop fusion | flops 131072 | bytes 786432 | tf_op jit(solution)/shard_map/convert_element_type | solution.py:165
  259.4 2.8 copy.49
  262.2 4.7 %fusion.20 = (f32[128]{0:T(128)S(1)}, f32[128]{0:T(128)S(1)}, f32[128,1024]{1,0:T(8,128)S(1)}) fusion(f32[1,16,8,1024]{3,1,2,0:T(8,128)S(1)} %copy.49, bf16[128,4096]{1,0:T(8,128)(2,1)S(1)} %bitcast.108, bf16[4096,1024]{1,0:T(8,128)(2,1)} %all-gather.6.cloned.1.call-done), kind=kOutput, calls=%fused_computation.31 | convolution fusion | flops 1074265856 | bytes 10486784 | tf_op jit(solution)/shard_map/dot_general | solution.py:167
  267.0 9.9 %all_to_all.50 = f32[8,1,384]{2,1,0:T(1,128)S(1)} all-to-all(f32[8,1,384]{2,1,0:T(1,128)S(1)} %broadcast_in_dim.42), channel_id=1, replica_groups=mesh['section'=8,'tp'=16] {'section'}, dimensions={0} | all-to-all | bytes 24576 | tf_op jit(solution)/shard_map/all_to_all | solution.py:21
  278.3 7.3 %copy.54 = bf16[8,16,4096]{1,0,2:T(8,128)(2,1)} copy(bf16[8,16,4096]{2,1,0:T(8,128)(2,1)S(1)} %bitcast.109) | data formatting | bytes 2097152 | tf_op jit(solution)/shard_map/reshape | solution.py:27
  285.7 10.5 %reshape.125 = bf16[16,2,16384]{2,1,0:T(2,128)(2,1)S(1)} reshape(bf16[4096,8,16]{2,1,0:T(8,128)(2,1)} %bitcast.103) | data formatting | bytes 2097152
  296.2 31.7 %all_to_all.51 = bf16[16,2,16384]{2,1,0:T(2,128)(2,1)S(1)} all-to-all(bf16[16,2,16384]{2,1,0:T(2,128)(2,1)S(1)} %reshape.125), channel_id=1, replica_groups=mesh['section'=8,'tp'=16] {'tp'}, dimensions={0} | all-to-all | bytes 2097152 | tf_op jit(solution)/shard_map/all_to_all | solution.py:187
  327.8 1.2 broadcast_in_dim.43
  329.1 5.7 %all-to-all-start.3 = ((f32[16,1,1]{2,1,0:T(1,128)}), f32[16,1,1]{2,1,0:T(1,128)S(1)}, u32[]{:S(2)}, u32[]{:S(2)}) async-start(f32[16,1,1]{2,1,0:T(1,128)} %broadcast_in_dim.43), calls=%async_computation.4 | async-start | bytes 16384 | tf_op jit(solution)/shard_map/all_to_all | solution.py:21
  334.8 7.2 %convolution_convert_fusion.1 = bf16[128,4096]{1,0:T(8,128)(2,1)} fusion(bf16[128,1024]{1,0:T(8,128)(2,1)S(1)} %copy-done.2, bf16[4096,1024]{1,0:T(8,128)(2,1)} %all-gather.6.cloned.1.call-done), kind=kOutput, calls=%fused_computation.4 | convolution fusion | flops 1074266112 | bytes 9699328 | tf_op jit(solution)/shard_map/dot_general | solution.py:181
  342.0 3.6 all-to-all-start.4
  345.6 7.5 %reshape.126 = bf16[4096,8,16]{2,1,0:T(8,128)(2,1)} reshape(bf16[16,2,16384]{2,1,0:T(2,128)(2,1)S(1)} %all_to_all.51) | data formatting | bytes 2097152
  353.1 8.3 %copy.56 = bf16[8,16,16,256]{3,2,1,0:T(8,128)(2,1)S(1)} copy(bf16[8,16,16,256]{2,0,3,1:T(8,128)(2,1)} %bitcast.104) | data formatting | bytes 2097152 | tf_op jit(solution)/shard_map/all_to_all | solution.py:187
  363.5 3.5 convolution_bitcast_fusion
  367.0 1.3 copy.57
  (50 shorter events, 7.3 us)
Async XLA Ops:
  7.2 66.6 %copy-start.3 = (bf16[1,2,8192,64]{2,3,1,0:T(8,128)(2,1)S(1)}, bf16[1,2,8192,64]{2,3,1,0:T(8,128)(2,1)}, u32[]{:S(2)}) copy-start(bf16[1,2,8192,64]{2,3,1,0:T(8,128)(2,1)} %param.11) | copy-start | bytes 6291460
  7.2 62.2 %all-gather.4.cloned.1.call-start = ((), (), s32[]{:S(2)}) async-start(), calls=%async_computation.7 | async-start | bytes 4456448 | tf_op jit(solution)/shard_map/all_gather | solution.py:129
  10.3 153.4 %reduce-scatter.2.cloned.1.call-start = ((), (), s32[]{:S(2)}) async-start(), calls=%async_computation.8 | async-start | bytes 4456448 | tf_op jit(solution)/shard_map/reduce_scatter | solution.py:150
  69.4 4.4 %copy-start = (bf16[256,8192]{1,0:T(8,128)(2,1)S(1)}, bf16[256,8192]{1,0:T(8,128)(2,1)}, u32[]{:S(2)}) copy-start(bf16[256,8192]{1,0:T(8,128)(2,1)} %all-gather.4.cloned.1.call-done) | copy-start | bytes 12582916
  73.4 7.9 %collective-permute-start.1 = (bf16[256,64]{0,1:T(8,128)(2,1)S(1)}, bf16[256,64]{0,1:T(8,128)(2,1)S(1)}, u32[]{:S(2)}, u32[]{:S(2)}) collective-permute-start(bf16[256,64]{0,1:T(8,128)(2,1)S(1)} %convolution_convert_fusion.3), channel_id=1, source_target_pairs={{0,1},{1,0},{2,3},{3,2},{4,5},{5,4},{6,7},{7,6},{8,9},{9,8},{10,11... | collective-permute-start | bytes 98312 | tf_op jit(solution)/shard_map/ppermute | solution.py:16
  73.8 8.6 %slice-start = ((s8[8388608]{0:T(1024)(128)(4,1)}), s8[4194304]{0:T(1024)(128)(4,1)S(1)}, s32[]{:S(2)}) async-start(s8[8388608]{0:T(1024)(128)(4,1)} %bitcast.110), calls=%async_computation.11 | async-start | bytes 8388608
  75.2 7.2 %slice-start.1 = ((s8[8388608]{0:T(1024)(128)(4,1)}), s8[4194304]{0:T(1024)(128)(4,1)S(1)}, s32[]{:S(2)}) async-start(s8[8388608]{0:T(1024)(128)(4,1)} %bitcast.110), calls=%async_computation.12 | async-start | bytes 8388608
  75.2 6.8 %collective-permute-start = (bf16[256,64]{0,1:T(8,128)(2,1)S(1)}, bf16[256,64]{0,1:T(8,128)(2,1)S(1)}, u32[]{:S(2)}, u32[]{:S(2)}) collective-permute-start(bf16[256,64]{0,1:T(8,128)(2,1)S(1)} %convolution_convert_fusion.4), channel_id=1, source_target_pairs={{0,1},{1,0},{2,3},{3,2},{4,5},{5,4},{6,7},{7,6},{8,9},{9,8},{10,11... | collective-permute-start | bytes 98312 | tf_op jit(solution)/shard_map/ppermute | solution.py:16
  86.9 76.8 %copy-start.1 = (bf16[1,16,8192]{2,1,0:T(8,128)(2,1)S(1)}, bf16[1,16,8192]{2,1,0:T(8,128)(2,1)}, u32[]{:S(2)}) copy-start(bf16[1,16,8192]{2,1,0:T(8,128)(2,1)} %param.8) | copy-start | bytes 786436
  86.9 175.3 %all-gather.6.cloned.1.call-start = ((), (), s32[]{:S(2)}) async-start(), calls=%async_computation.9 | async-start | bytes 8912896 | tf_op jit(solution)/shard_map/all_gather | solution.py:166
  164.7 52.5 %copy-start.4 = (bf16[1,16,8192]{2,1,0:T(8,128)(2,1)}, bf16[1,16,8192]{2,1,0:T(8,128)(2,1)S(1)}, u32[]{:S(2)}) copy-start(bf16[1,16,8192]{2,1,0:T(8,128)(2,1)S(1)} %fusion.26) | copy-start | bytes 786436
  172.0 58.1 %copy-start.5 = (bf16[1,16,4096]{2,1,0:T(8,128)(2,1)S(1)}, bf16[1,16,4096]{2,1,0:T(8,128)(2,1)}, u32[]{:S(2)}) copy-start(bf16[1,16,4096]{2,1,0:T(8,128)(2,1)} %param.14) | copy-start | bytes 393220
  231.2 31.0 %all-to-all-start = ((bf16[8,1,16,4096]{3,2,1,0:T(8,128)(2,1)}), bf16[8,1,16,4096]{3,2,1,0:T(8,128)(2,1)S(1)}, u32[]{:S(2)}, u32[]{:S(2)}) async-start(bf16[8,1,16,4096]{3,2,1,0:T(8,128)(2,1)} %broadcast_in_dim.41), calls=%async_computation.1 | async-start | bytes 2097152 | tf_op jit(solution)/shard_map/all_to_all | solution.py:21
  234.7 128.8 %all-gather.8.cloned.1.call-start = ((), (), s32[]{:S(2)}) async-start(), calls=%async_computation.10 | async-start | bytes 4456448 | tf_op jit(solution)/shard_map/all_gather | solution.py:192
  285.7 49.1 %copy-start.2 = (bf16[128,1024]{1,0:T(8,128)(2,1)S(1)}, bf16[128,1024]{1,0:T(8,128)(2,1)}, u32[]{:S(2)}) copy-start(bf16[128,1024]{1,0:T(8,128)(2,1)} %fusion.23) | copy-start | bytes 786436
  329.1 12.9 %all-to-all-start.3 = ((f32[16,1,1]{2,1,0:T(1,128)}), f32[16,1,1]{2,1,0:T(1,128)S(1)}, u32[]{:S(2)}, u32[]{:S(2)}) async-start(f32[16,1,1]{2,1,0:T(1,128)} %broadcast_in_dim.43), calls=%async_computation.4 | async-start | bytes 16384 | tf_op jit(solution)/shard_map/all_to_all | solution.py:21
  342.0 20.7 %all-to-all-start.4 = ((bf16[8,16,4096]{2,1,0:T(8,128)(2,1)}), bf16[8,16,4096]{2,1,0:T(8,128)(2,1)S(1)}, u32[]{:S(2)}, u32[]{:S(2)}) async-start(bf16[8,16,4096]{2,1,0:T(8,128)(2,1)} %bitcast.25), calls=%async_computation.5 | async-start | bytes 2097152 | tf_op jit(solution)/shard_map/all_to_all | solution.py:56
Sparse Core Ops, SparseCore 0:
  11.0 58.3 all-gather.3
  87.0 76.6 reduce-scatter.1
  166.2 73.9 all-gather.5
  278.5 63.0 all-gather.7
where the time goes:
time: 377 us; the launch traced here: 376 us
  waiting for transfers between devices  135 us (36%)
  other arithmetic  72 us (19%)
  local copies, waits for them, and re-layouts  54.7 us (15%)
  blocking collectives  52.1 us (14%)
  matrix products  32 us (8%)
  between operations  16.4 us (4%)
  starting transfers between devices  13.8 us (4%)
    reduce_scatter x1, waiting for transfers between devices, shards(): lax.psum_scatter(round_bf16(jnp.dot(block, out_local, preferred_element_t...  76.1 us
    all_gather x1, waiting for transfers between devices, shards(): block_rows = lax.all_gather(normed, 'tp', axis=0, tiled=True)  58.2 us
    unnamed x2, other arithmetic  45.3 us
    all_to_all x1, blocking collectives, shards(): lax.all_to_all(gathered, 'tp', split_axis=2, concat_axis=1, tiled=True)  31.7 us
    unnamed x22, local copies, waits for them, and re-layouts  27.2 us
    all_to_all x1, blocking collectives, shards(): lax.all_to_all(teacher_next[None], 'section', split_axis=2, concat_axis=0...  10.6 us
    all_to_all x1, blocking collectives, from_everyone(): return lax.all_to_all(copies, axis, split_axis=0, concat_axis=0, tiled=True)  9.85 us
    all_to_all x2, starting transfers between devices, from_everyone(): return lax.all_to_all(copies, axis, split_axis=0, concat_axis=0, tiled=True)  9.24 us
  transfers between devices with their start and end apart: 9, of which 2 were waited for; matrix products, arithmetic and copies ran while one was open for 36% of the time, Pallas kernels for 0%

commit v1 on v0

--- a/solution.py
+++ b/solution.py
@@ -184,7 +184,10 @@
         "section",
         0,
     )
-    by_column = lax.all_to_all(gathered, "tp", split_axis=2, concat_axis=1, tiled=True)
+    by_column = jnp.concatenate(
+        lax.all_to_all(jnp.stack(jnp.split(gathered, lax.axis_size("tp"), axis=2)), "tp", 0, 0),
+        axis=1,
+    )
     slope_stacked = slope.reshape(gathered.shape[0], gathered.shape[1], slope.shape[1])
     block = by_column
     grad_proj = lax.dot_general(

time: 377 us -> 357 us (0.947)
  local copies, waits for them, and re-layouts: 54.7 us -> 20.1 us
  waiting for transfers between devices: 135 us -> 150 us
    unnamed x22 -> x34, local copies, waits for them, and re-layouts: 27.2 us -> 8.03 us
    all_to_all x1, waiting for transfers between devices: 0.01 us -> 15.4 us  [sent_and_summed(): lax.all_to_all(pieces, axis, split_axis=0, concat_axis=0, tiled=True)]
    all_to_all x1 -> x0, local copies, waits for them, and re-layouts: 8.27 us -> none  [shards(): lax.all_to_all(gathered, 'tp', split_axis=2, concat_axis=1, tiled=True)]
    reshape x1, local copies, waits for them, and re-layouts: 7.32 us -> 0.09 us  [shards(): jnp.concatenate(lax.all_to_all(jnp.stack(jnp.split(gathered, lax.axis_siz...]
  transfers between devices with their start and end apart: 9 -> 9, of which waited for: 2 -> 3; matrix products, arithmetic and copies ran while one was open for 36% -> 29% of each run, Pallas kernels for 0% -> 0%
where the time goes in v1:
time: 357 us; the launch traced here: 356 us
  waiting for transfers between devices  150 us (42%)
  other arithmetic  72 us (20%)
  blocking collectives  50.1 us (14%)
  matrix products  33.5 us (9%)
  local copies, waits for them, and re-layouts  20.1 us (6%)
  between operations  16.5 us (5%)
  starting transfers between devices  13.2 us (4%)
    reduce_scatter x1, waiting for transfers between devices, shards(): lax.psum_scatter(round_bf16(jnp.dot(block, out_local, preferred_element_t...  76.1 us
    all_gather x1, waiting for transfers between devices, shards(): block_rows = lax.all_gather(normed, 'tp', axis=0, tiled=True)  58.2 us
    unnamed x2, other arithmetic  45.3 us
    all_to_all x1, blocking collectives, shards(): lax.all_to_all(jnp.stack(jnp.split(gathered, lax.axis_size('tp'), axis=2)...  29.6 us
    all_to_all x1, waiting for transfers between devices, sent_and_summed(): lax.all_to_all(pieces, axis, split_axis=0, concat_axis=0, tiled=True)  15.4 us
    all_to_all x1, blocking collectives, shards(): lax.all_to_all(teacher_next[None], 'section', split_axis=2, concat_axis=0...  10.6 us
    all_to_all x1, blocking collectives, from_everyone(): return lax.all_to_all(copies, axis, split_axis=0, concat_axis=0, tiled=True)  9.85 us
    all_to_all x2, starting transfers between devices, from_everyone(): return lax.all_to_all(copies, axis, split_axis=0, concat_axis=0, tiled=True)  8.58 us
  transfers between devices with their start and end apart: 9, of which 3 were waited for; matrix products, arithmetic and copies ran while one was open for 29% of the time, Pallas kernels for 0%

profile of v1, /device:TPU:1, one launch (start us, length us, event | category | flops | bytes accessed | tf_op | source)
XLA Modules:
  0.0 355.6 jit_solution(1296914501224784408)
XLA Ops:
  7.2 1.3 fusion.16
  8.5 1.8 fusion.18
  11.2 58.2 %all-gather.4.cloned.1.call-done = bf16[256,8192]{1,0:T(8,128)(2,1)} async-done(((bf16[16,8192]{1,0:T(8,128)(2,1)}), bf16[256,8192]{1,0:T(8,128)(2,1)}) %all-gather.4.cloned.1.call-update) | async-done | bytes 4194320 | tf_op jit(solution)/shard_map/all_gather | solution.py:129
  69.4 4.0 %convolution_convert_fusion.3 = bf16[256,64]{0,1:T(8,128)(2,1)S(1)} fusion(bf16[256,8192]{1,0:T(8,128)(2,1)} %all-gather.4.cloned.1.call-done, bf16[1,2,8192,64]{2,3,1,0:T(8,128)(2,1)} %param.11), kind=kOutput, calls=%fused_computation.13 | convolution fusion | flops 268451840 | bytes 5275648 | tf_op jit(solution)/shard_map/dot_general | solution.py:133
  73.8 1.4 convolution_convert_fusion.4
  75.5 5.8 %fusion.8 = bf16[32,4,8,128]{3,2,1,0:T(8,128)(2,1)S(1)} fusion(bf16[256,8192]{1,0:T(8,128)(2,1)S(1)} %copy-done, bf16[1,8192,512]{2,1,0:T(8,128)(2,1)} %param.10), kind=kOutput, calls=%fused_computation.12 | convolution fusion | flops 2147614720 | bytes 12845056 | tf_op jit(solution)/shard_map/dot_general | solution.py:130
  82.4 4.5 %convolution_convert_fusion = bf16[256,8192]{1,0:T(8,128)(2,1)} fusion(bf16[256,512]{0,1:T(8,128)(2,1)S(1)} %bitcast.186, bf16[1,512,8192]{2,1,0:T(8,128)(2,1)S(1)} %bitcast.181), kind=kOutput, calls=%fused_computation | convolution fusion | flops 2149580800 | bytes 12845056 | tf_op jit(solution)/shard_map/dot_general | solution.py:151
  87.6 76.1 %reduce-scatter.2.cloned.1.call-done = bf16[16,8192]{1,0:T(8,128)(2,1)} async-done(((bf16[256,8192]{1,0:T(8,128)(2,1)}), bf16[16,8192]{1,0:T(8,128)(2,1)}) %reduce-scatter.2.cloned.1.call-update) | async-done | bytes 262160 | tf_op jit(solution)/shard_map/reduce_scatter | solution.py:150
  163.7 1.0 fusion.26
  164.7 6.8 %copy.59 = bf16[1,16,8192]{1,0,2:T(2,128)(2,1)} copy(bf16[1,16,8192]{2,1,0:T(8,128)(2,1)S(1)} %fusion.26) | data formatting | bytes 524288 | tf_op jit(solution)/shard_map/broadcast_in_dim | solution.py:199
  172.0 45.2 %reduce.8 = bf16[8192,16]{1,0:T(8,128)(2,1)S(1)} reduce(bf16[8192,1,16]{2,1,0:T(2,128)(2,1)} %bitcast.161, bf16[]{:T(256)} %broadcast.68), dimensions={1}, to_apply=%bitcast.141.reduce_sub_computation | reduce | bytes 524290
  217.3 2.2 reshape.131
  219.5 10.6 %all_to_all.36 = bf16[8,2,8192]{2,1,0:T(2,128)(2,1)S(1)} all-to-all(bf16[8,2,8192]{2,1,0:T(2,128)(2,1)S(1)} %reshape.131), channel_id=1, replica_groups=mesh['section'=8,'tp'=16] {'section'}, dimensions={0} | all-to-all | bytes 524288 | tf_op jit(solution)/shard_map/all_to_all | solution.py:164
  230.1 1.1 broadcast_in_dim.41
  231.2 3.6 %all-to-all-start = ((bf16[8,1,16,4096]{3,2,1,0:T(8,128)(2,1)}), bf16[8,1,16,4096]{3,2,1,0:T(8,128)(2,1)S(1)}, u32[]{:S(2)}, u32[]{:S(2)}) async-start(bf16[8,1,16,4096]{3,2,1,0:T(8,128)(2,1)} %broadcast_in_dim.41), calls=%async_computation.1 | async-start | bytes 2097152 | tf_op jit(solution)/shard_map/all_to_all | solution.py:21
  234.8 5.1 %reshape.132 = bf16[8192,1,16]{2,1,0:T(2,128)(2,1)} reshape(bf16[8,2,8192]{2,1,0:T(2,128)(2,1)S(1)} %all_to_all.36) | data formatting | bytes 524288
  239.9 8.5 %convert_multiply_fusion.2 = f32[1,16,8192]{1,0,2:T(1,128)} fusion(bf16[8192,1,16]{2,1,0:T(2,128)(2,1)} %reshape.132), kind=kLoop, calls=%fused_computation.100 | loop fusion | flops 262144 | bytes 786432 | tf_op jit(solution)/shard_map/mul | solution.py:172
  248.4 2.5 reduce_sum.89
  250.9 8.5 %bitcast_convert_fusion = f32[1,16,8192]{1,0,2:T(1,128)} fusion(bf16[8192,1,16]{2,1,0:T(2,128)(2,1)} %reshape.132), kind=kLoop, calls=%fused_computation.104 | loop fusion | flops 131072 | bytes 786432 | tf_op jit(solution)/shard_map/convert_element_type | solution.py:165
  259.4 2.8 copy.60
  262.2 4.7 %fusion.20 = (f32[128]{0:T(128)S(1)}, f32[128]{0:T(128)S(1)}, f32[128,1024]{1,0:T(8,128)S(1)}) fusion(f32[1,16,8,1024]{3,1,2,0:T(8,128)S(1)} %copy.60, bf16[128,4096]{1,0:T(8,128)(2,1)S(1)} %bitcast.163, bf16[4096,1024]{1,0:T(8,128)(2,1)} %all-gather.6.cloned.1.call-done), kind=kOutput, calls=%fused_computation.31 | convolution fusion | flops 1074265856 | bytes 10486784 | tf_op jit(solution)/shard_map/dot_general | solution.py:167
  267.0 9.9 %all_to_all.37 = f32[8,1,384]{2,1,0:T(1,128)S(1)} all-to-all(f32[8,1,384]{2,1,0:T(1,128)S(1)} %broadcast_in_dim.42), channel_id=1, replica_groups=mesh['section'=8,'tp'=16] {'section'}, dimensions={0} | all-to-all | bytes 24576 | tf_op jit(solution)/shard_map/all_to_all | solution.py:21
  277.5 0.9 fusion.23
  278.7 29.6 %all_to_all.38 = bf16[16,8,16,256]{3,2,1,0:T(8,128)(2,1)S(1)} all-to-all(bf16[16,8,16,256]{3,2,1,0:T(8,128)(2,1)S(1)} %fusion.30), channel_id=1, replica_groups=mesh['section'=8,'tp'=16] {'tp'}, dimensions={0} | all-to-all | bytes 2097152 | tf_op jit(solution)/shard_map/all_to_all | solution.py:188
  308.3 1.2 broadcast_in_dim.43
  309.5 5.0 %all-to-all-start.3 = ((f32[16,1,1]{2,1,0:T(1,128)}), f32[16,1,1]{2,1,0:T(1,128)S(1)}, u32[]{:S(2)}, u32[]{:S(2)}) async-start(f32[16,1,1]{2,1,0:T(1,128)} %broadcast_in_dim.43), calls=%async_computation.4 | async-start | bytes 16384 | tf_op jit(solution)/shard_map/all_to_all | solution.py:21
  314.5 7.8 %convolution_convert_fusion.1 = bf16[128,4096]{1,0:T(8,128)(2,1)} fusion(bf16[128,1024]{1,0:T(8,128)(2,1)S(1)} %copy-done.2, bf16[4096,1024]{1,0:T(8,128)(2,1)} %all-gather.6.cloned.1.call-done), kind=kOutput, calls=%fused_computation.4 | convolution fusion | flops 1074266112 | bytes 9699328 | tf_op jit(solution)/shard_map/dot_general | solution.py:181
  322.3 3.6 %all-to-all-start.4 = ((bf16[8,16,4096]{2,1,0:T(8,128)(2,1)}), bf16[8,16,4096]{2,1,0:T(8,128)(2,1)S(1)}, u32[]{:S(2)}, u32[]{:S(2)}) async-start(bf16[8,16,4096]{2,1,0:T(8,128)(2,1)} %bitcast.25), calls=%async_computation.5 | async-start | bytes 2097152 | tf_op jit(solution)/shard_map/all_to_all | solution.py:56
  326.0 0.6 reduce_sum.94
  327.2 15.4 %all-to-all-done.4 = bf16[8,16,4096]{2,1,0:T(8,128)(2,1)S(1)} async-done(((bf16[8,16,4096]{2,1,0:T(8,128)(2,1)}), bf16[8,16,4096]{2,1,0:T(8,128)(2,1)S(1)}, u32[]{:S(2)}, u32[]{:S(2)}) %all-to-all-start.4) | async-done | bytes 1048608 | tf_op jit(solution)/shard_map/all_to_all | solution.py:56
  342.7 0.8 convert_reduce_fusion
  343.5 4.4 %convolution_bitcast_fusion = f32[256,1024]{1,0:T(8,128)} fusion(bf16[8,256,256]{2,1,0:T(8,128)(2,1)S(1)} %bitcast.182, bf16[8,256,1024]{2,1,0:T(8,128)(2,1)} %all-gather.8.cloned.1.call-done), kind=kOutput, calls=%fused_computation.6 | convolution fusion | flops 1073741824 | bytes 6291456 | tf_op jit(solution)/shard_map/dot_general | solution.py:193
  (62 shorter events, 4.2 us)
Async XLA Ops:
  7.2 66.6 %copy-start.3 = (bf16[1,2,8192,64]{2,3,1,0:T(8,128)(2,1)S(1)}, bf16[1,2,8192,64]{2,3,1,0:T(8,128)(2,1)}, u32[]{:S(2)}) copy-start(bf16[1,2,8192,64]{2,3,1,0:T(8,128)(2,1)} %param.11) | copy-start | bytes 6291460
  7.2 62.2 %all-gather.4.cloned.1.call-start = ((), (), s32[]{:S(2)}) async-start(), calls=%async_computation.7 | async-start | bytes 4456448 | tf_op jit(solution)/shard_map/all_gather | solution.py:129
  10.3 153.4 %reduce-scatter.2.cloned.1.call-start = ((), (), s32[]{:S(2)}) async-start(), calls=%async_computation.8 | async-start | bytes 4456448 | tf_op jit(solution)/shard_map/reduce_scatter | solution.py:150
  69.4 4.4 %copy-start = (bf16[256,8192]{1,0:T(8,128)(2,1)S(1)}, bf16[256,8192]{1,0:T(8,128)(2,1)}, u32[]{:S(2)}) copy-start(bf16[256,8192]{1,0:T(8,128)(2,1)} %all-gather.4.cloned.1.call-done) | copy-start | bytes 12582916
  73.4 7.9 %collective-permute-start.1 = (bf16[256,64]{0,1:T(8,128)(2,1)S(1)}, bf16[256,64]{0,1:T(8,128)(2,1)S(1)}, u32[]{:S(2)}, u32[]{:S(2)}) collective-permute-start(bf16[256,64]{0,1:T(8,128)(2,1)S(1)} %convolution_convert_fusion.3), channel_id=1, source_target_pairs={{0,1},{1,0},{2,3},{3,2},{4,5},{5,4},{6,7},{7,6},{8,9},{9,8},{10,11... | collective-permute-start | bytes 98312 | tf_op jit(solution)/shard_map/ppermute | solution.py:16
  73.8 8.6 %slice-start = ((s8[8388608]{0:T(1024)(128)(4,1)}), s8[4194304]{0:T(1024)(128)(4,1)S(1)}, s32[]{:S(2)}) async-start(s8[8388608]{0:T(1024)(128)(4,1)} %bitcast.180), calls=%async_computation.11 | async-start | bytes 8388608
  75.2 7.2 %slice-start.1 = ((s8[8388608]{0:T(1024)(128)(4,1)}), s8[4194304]{0:T(1024)(128)(4,1)S(1)}, s32[]{:S(2)}) async-start(s8[8388608]{0:T(1024)(128)(4,1)} %bitcast.180), calls=%async_computation.12 | async-start | bytes 8388608
  75.2 6.8 %collective-permute-start = (bf16[256,64]{0,1:T(8,128)(2,1)S(1)}, bf16[256,64]{0,1:T(8,128)(2,1)S(1)}, u32[]{:S(2)}, u32[]{:S(2)}) collective-permute-start(bf16[256,64]{0,1:T(8,128)(2,1)S(1)} %convolution_convert_fusion.4), channel_id=1, source_target_pairs={{0,1},{1,0},{2,3},{3,2},{4,5},{5,4},{6,7},{7,6},{8,9},{9,8},{10,11... | collective-permute-start | bytes 98312 | tf_op jit(solution)/shard_map/ppermute | solution.py:16
  86.9 76.8 %copy-start.1 = (bf16[1,16,8192]{2,1,0:T(8,128)(2,1)S(1)}, bf16[1,16,8192]{2,1,0:T(8,128)(2,1)}, u32[]{:S(2)}) copy-start(bf16[1,16,8192]{2,1,0:T(8,128)(2,1)} %param.8) | copy-start | bytes 786436
  86.9 175.3 %all-gather.6.cloned.1.call-start = ((), (), s32[]{:S(2)}) async-start(), calls=%async_computation.9 | async-start | bytes 8912896 | tf_op jit(solution)/shard_map/all_gather | solution.py:166
  164.7 6.8 %copy-start.4 = (bf16[1,16,8192]{2,1,0:T(8,128)(2,1)}, bf16[1,16,8192]{2,1,0:T(8,128)(2,1)S(1)}, u32[]{:S(2)}) copy-start(bf16[1,16,8192]{2,1,0:T(8,128)(2,1)S(1)} %fusion.26) | copy-start | bytes 786436
  172.0 58.1 %copy-start.5 = (bf16[1,16,4096]{2,1,0:T(8,128)(2,1)S(1)}, bf16[1,16,4096]{2,1,0:T(8,128)(2,1)}, u32[]{:S(2)}) copy-start(bf16[1,16,4096]{2,1,0:T(8,128)(2,1)} %param.14) | copy-start | bytes 393220
  231.2 31.0 %all-to-all-start = ((bf16[8,1,16,4096]{3,2,1,0:T(8,128)(2,1)}), bf16[8,1,16,4096]{3,2,1,0:T(8,128)(2,1)S(1)}, u32[]{:S(2)}, u32[]{:S(2)}) async-start(bf16[8,1,16,4096]{3,2,1,0:T(8,128)(2,1)} %broadcast_in_dim.41), calls=%async_computation.1 | async-start | bytes 2097152 | tf_op jit(solution)/shard_map/all_to_all | solution.py:21
  234.7 108.8 %all-gather.8.cloned.1.call-start = ((), (), s32[]{:S(2)}) async-start(), calls=%async_computation.10 | async-start | bytes 4456448 | tf_op jit(solution)/shard_map/all_gather | solution.py:195
  278.3 36.2 %copy-start.2 = (bf16[128,1024]{1,0:T(8,128)(2,1)S(1)}, bf16[128,1024]{1,0:T(8,128)(2,1)}, u32[]{:S(2)}) copy-start(bf16[128,1024]{1,0:T(8,128)(2,1)} %fusion.23) | copy-start | bytes 786436
  309.5 12.8 %all-to-all-start.3 = ((f32[16,1,1]{2,1,0:T(1,128)}), f32[16,1,1]{2,1,0:T(1,128)S(1)}, u32[]{:S(2)}, u32[]{:S(2)}) async-start(f32[16,1,1]{2,1,0:T(1,128)} %broadcast_in_dim.43), calls=%async_computation.4 | async-start | bytes 16384 | tf_op jit(solution)/shard_map/all_to_all | solution.py:21
  322.3 20.4 %all-to-all-start.4 = ((bf16[8,16,4096]{2,1,0:T(8,128)(2,1)}), bf16[8,16,4096]{2,1,0:T(8,128)(2,1)S(1)}, u32[]{:S(2)}, u32[]{:S(2)}) async-start(bf16[8,16,4096]{2,1,0:T(8,128)(2,1)} %bitcast.25), calls=%async_computation.5 | async-start | bytes 2097152 | tf_op jit(solution)/shard_map/all_to_all | solution.py:56
Sparse Core Ops, SparseCore 0:
  11.0 58.3 all-gather.3
  87.0 76.6 reduce-scatter.1
  166.2 73.9 all-gather.5
  278.5 60.6 all-gather.7
